TPU v7x, 128 devices: a whole 4x4x4 slice. The times are simulated.
128 devices in a mesh: space: 8 (over y_lo, z), tm: 16 (over y_hi, x, core).
Axes of the slice: x: 4, y: 4 (y_hi: 2, y_lo: 2; y = y_hi * 2 + y_lo), z: 4, core: 2. Of those that a mesh axis runs over, the one named last changes fastest.
Arguments:
- coefficients: float32 [2048, 8192], P('tm', 'space'), may hold values from -6 to 6
- counts: int32 [2048, 8192], P('tm', 'space'), may hold values from 0 to 2
- coords: float32 [2, 8192], replicated, may hold values from 0 to 12
- pattern: int32 [64, 8], replicated, may hold values from 0 to 63, as said below
- temporal_taps: float32 [9], replicated, may hold values from 0.05 to 0.35
Outputs:
- newton_step: float32 [2048, 8192], P('tm', 'space')
- residual: float32 [2048, 8192], P('tm', 'space')
Inputs may be any that keep to these rules, and one draw needn't show every extreme that they name: `pattern`: each row lists 8 distinct block indices including the row's own index, and block j appears in row i exactly when block i appears in row j.
All inputs are finite; a program needn't handle non-finite values.
Results may differ from a plain program's by a relative error of at most 0.00016.
Values sent between devices are 32-bit elements; how exact they have to be, the bound alone decides.
A program may use at most 64 MiB of HBM per device.

v0:
```python
import jax
import jax.numpy as jnp
from jax import lax
from jax.sharding import PartitionSpec as P

BLOCK = 128
BW = 8
ITERS = 2


support = 0.25
amplitude = 0.2
row_group = 16


def with_halo(block, sides, width):
    for axis, dim in sides:
        count = lax.axis_size(axis)
        forward = [(i, i + 1) for i in range(count - 1)]
        backward = [(target, source) for source, target in forward]
        low = lax.ppermute(
            lax.slice_in_dim(block, block.shape[dim] - width, None, axis=dim), axis, forward
        )
        high = lax.ppermute(lax.slice_in_dim(block, 0, width, axis=dim), axis, backward)
        block = jnp.concatenate([low, block, high], axis=dim)
    return block


def wendland(distance):
    scaled = distance / support
    remain = jnp.maximum(1.0 - scaled, 0.0)
    return amplitude * remain**4 * (1.0 + 4.0 * scaled)


def band_product(field, temporal_taps):
    length = field.shape[0]
    padded = with_halo(field, (("tm", 0),), BW)
    summed = temporal_taps[0] * field
    for offset in range(1, BW + 1):
        summed = summed + temporal_taps[offset] * (
            padded[BW - offset : BW - offset + length] + padded[BW + offset : BW + offset + length]
        )
    return summed


def block_product(field, coords, pattern):
    day_count = field.shape[0]
    blocks = pattern.shape[0]
    blocked = field.reshape(day_count, blocks, BLOCK)
    located = coords.reshape(2, blocks, BLOCK)

    def group_out(first_row):
        row_ids = first_row + jnp.arange(row_group)
        columns = pattern[row_ids]
        row_coords = located[:, row_ids]
        col_coords = located[:, columns]
        delta_x = row_coords[0][:, None, :, None] - col_coords[0][:, :, None, :]
        delta_y = row_coords[1][:, None, :, None] - col_coords[1][:, :, None, :]
        weight = wendland(jnp.sqrt(delta_x * delta_x + delta_y * delta_y))
        picked = blocked[:, columns]
        return jnp.einsum("rjab,drjb->dra", weight, picked, precision=lax.Precision.HIGHEST)

    starts = jnp.arange(blocks // row_group) * row_group
    outputs = lax.map(group_out, starts)
    return outputs.transpose(1, 0, 2, 3).reshape(day_count, blocks * BLOCK)


def to_days(field):
    return lax.all_to_all(field, "space", split_axis=0, concat_axis=1, tiled=True)


def to_cells(field):
    return lax.all_to_all(field, "space", split_axis=1, concat_axis=0, tiled=True)


def residual_norm(residual):
    return lax.psum(jnp.sum(residual * residual), ("space", "tm"))


def shards(coefficients, counts, coords, pattern, temporal_taps):

    def spatial_days(field):
        return block_product(to_days(band_product(field, temporal_taps)), coords, pattern)

    def spread(field):
        return to_cells(spatial_days(field))

    latent_days = spatial_days(coefficients)
    latent = to_cells(latent_days)
    intensity = jnp.exp(latent)
    gradient = coefficients + spread(intensity - counts.astype(jnp.float32))
    residual = -gradient
    direction = residual
    newton_step = jnp.zeros_like(residual)
    norm_now = residual_norm(residual)
    for iteration in range(ITERS):
        image = spread(direction)
        weighted = intensity * image
        curved = direction + spread(weighted)
        curvature = lax.psum(jnp.sum(direction * curved), ("space", "tm"))
        step_size = norm_now / curvature
        newton_step = newton_step + step_size * direction
        residual = residual - step_size * curved
        if iteration + 1 < ITERS:
            norm_next = residual_norm(residual)
            direction = residual + norm_next / norm_now * direction
            norm_now = norm_next
    return (newton_step, residual)


def solution(mesh):
    placed = (P("tm", "space"), P("tm", "space"), P(), P(), P())
    return jax.shard_map(
        shards,
        mesh=mesh,
        in_specs=placed,
        out_specs=(P("tm", "space"), P("tm", "space")),
        check_vma=False,
    )
```

profile of v0, /device:TPU:0, one launch (start us, length us, event | category | flops | bytes accessed | tf_op | source)
XLA Modules:
  0.0 868.4 jit_solution(1009812257972328115)
XLA Ops:
  7.7 7.3 fusion.413
  21.6 8.7 %all-to-all-done = f32[8,16,1024]{2,1,0:T(8,128)S(1)} async-done(((f32[8,16,1024]{2,1,0:T(8,128)}), f32[8,16,1024]{2,1,0:T(8,128)S(1)}, u32[]{:S(2)}, u32[]{:S(2)}) %all-to-all-start) | async-done | bytes 524320 | tf_op jit(solution)/shard_map/all_to_all | solution.py:69
  31.5 66.5 %while.72 = (s32[]{:T(128)}, f32[4,16,16,128]{3,1,2,0:T(8,128)S(1)}, s32[4]{0:T(128)S(1)}, s32[64,8]{1,0:T(8,128)S(1)}, f32[16,64,128]{2,0,1:T(8,128)S(1)}, /*index=5*/f32[2,64,128]{2,0,1:T(2,128)S(1)}, s32[]{:T(128)}) while((s32[]{:T(128)}, f32[4,16,16,128]{3,1,2,0:T(8,128)S(1)}, s32[4]{0:T(128)S(1)}, s32[64,8]{1,0:T(8,128)S(1)}, ...), condition=%wide.region_1.2_spmd, body=%wide.region_0.1_spmd.sunk | while | flops 432015808 | bytes 4029281 | solution.py:64
  36.0 12.2 %fusion.495 = f32[4,16,16,128]{3,1,2,0:T(8,128)S(1)} fusion(f32[4,16,16,128]{3,1,2,0:T(8,128)S(1)} %get-tuple-element.1017, s32[]{:T(128)} %get-tuple-element.1016, f32[16,16,8,128]{3,0,2,1:T(8,128)S(1)} %bitcast.397, f32[16,8,128]{2,1,0:T(8,128)S(1)} %bitcast.429, f32[16,128]{1,0:T(8,128)S(1)} %bitcast.441, f32[16,8,128]{2,1,0:T(8,128)S(1)} %bitcast.428, ...), kind=kOutput, calls=%fused_computation.50.clone.1 | convolution fusion | flops 432013312 | bytes 1327108 | tf_op jit(solution)/shard_map/while/body/eval_jaxpr/rjab,drjb->dra/dot_general | solution.py:61
  52.5 12.2 %fusion.495 = f32[4,16,16,128]{3,1,2,0:T(8,128)S(1)} fusion(f32[4,16,16,128]{3,1,2,0:T(8,128)S(1)} %get-tuple-element.1017, s32[]{:T(128)} %get-tuple-element.1016, f32[16,16,8,128]{3,0,2,1:T(8,128)S(1)} %bitcast.397, f32[16,8,128]{2,1,0:T(8,128)S(1)} %bitcast.429, f32[16,128]{1,0:T(8,128)S(1)} %bitcast.441, f32[16,8,128]{2,1,0:T(8,128)S(1)} %bitcast.428, ...), kind=kOutput, calls=%fused_computation.50.clone.1 | convolution fusion | flops 432013312 | bytes 1327108 | tf_op jit(solution)/shard_map/while/body/eval_jaxpr/rjab,drjb->dra/dot_general | solution.py:61
  69.0 12.2 %fusion.495 = f32[4,16,16,128]{3,1,2,0:T(8,128)S(1)} fusion(f32[4,16,16,128]{3,1,2,0:T(8,128)S(1)} %get-tuple-element.1017, s32[]{:T(128)} %get-tuple-element.1016, f32[16,16,8,128]{3,0,2,1:T(8,128)S(1)} %bitcast.397, f32[16,8,128]{2,1,0:T(8,128)S(1)} %bitcast.429, f32[16,128]{1,0:T(8,128)S(1)} %bitcast.441, f32[16,8,128]{2,1,0:T(8,128)S(1)} %bitcast.428, ...), kind=kOutput, calls=%fused_computation.50.clone.1 | convolution fusion | flops 432013312 | bytes 1327108 | tf_op jit(solution)/shard_map/while/body/eval_jaxpr/rjab,drjb->dra/dot_general | solution.py:61
  85.5 12.2 %fusion.495 = f32[4,16,16,128]{3,1,2,0:T(8,128)S(1)} fusion(f32[4,16,16,128]{3,1,2,0:T(8,128)S(1)} %get-tuple-element.1017, s32[]{:T(128)} %get-tuple-element.1016, f32[16,16,8,128]{3,0,2,1:T(8,128)S(1)} %bitcast.397, f32[16,8,128]{2,1,0:T(8,128)S(1)} %bitcast.429, f32[16,128]{1,0:T(8,128)S(1)} %bitcast.441, f32[16,8,128]{2,1,0:T(8,128)S(1)} %bitcast.428, ...), kind=kOutput, calls=%fused_computation.50.clone.1 | convolution fusion | flops 432013312 | bytes 1327108 | tf_op jit(solution)/shard_map/while/body/eval_jaxpr/rjab,drjb->dra/dot_general | solution.py:61
  98.7 15.6 %all_to_all.204 = f32[16,8,1024]{2,0,1:T(8,128)S(1)} all-to-all(f32[16,8,1024]{2,0,1:T(8,128)S(1)} %copy.119), channel_id=1, replica_groups=mesh['space'=8,'tm'=16] {'space'}, dimensions={1} | all-to-all | bytes 1048576 | tf_op jit(solution)/shard_map/all_to_all | solution.py:73
  122.0 7.1 fusion.370
  132.6 8.6 all-to-all-done.2
  141.9 66.1 %while.73 = (s32[]{:T(128)}, f32[4,16,16,128]{3,1,2,0:T(8,128)S(1)}, s32[4]{0:T(128)S(1)}, s32[64,8]{1,0:T(8,128)S(1)}, f32[16,64,128]{2,0,1:T(8,128)S(1)}, /*index=5*/f32[2,64,128]{2,0,1:T(2,128)S(1)}, s32[]{:T(128)}) while((s32[]{:T(128)}, f32[4,16,16,128]{3,1,2,0:T(8,128)S(1)}, s32[4]{0:T(128)S(1)}, s32[64,8]{1,0:T(8,128)S(1)}, ...), condition=%wide.region_3.4_spmd, body=%wide.region_2.3_spmd.sunk | while | flops 432015808 | bytes 4029281 | solution.py:64
  146.3 12.2 %fusion.501 = f32[4,16,16,128]{3,1,2,0:T(8,128)S(1)} fusion(f32[4,16,16,128]{3,1,2,0:T(8,128)S(1)} %get-tuple-element.1038, s32[]{:T(128)} %get-tuple-element.1037, f32[16,16,8,128]{3,0,2,1:T(8,128)S(1)} %bitcast.398, f32[16,8,128]{2,1,0:T(8,128)S(1)} %bitcast.431, f32[16,128]{1,0:T(8,128)S(1)} %bitcast.443, f32[16,8,128]{2,1,0:T(8,128)S(1)} %bitcast.430, ...), kind=kOutput, calls=%fused_computation.87.clone.1 | convolution fusion | flops 432013312 | bytes 1327108 | tf_op jit(solution)/shard_map/while/body/eval_jaxpr/rjab,drjb->dra/dot_general | solution.py:61
  162.7 12.2 %fusion.501 = f32[4,16,16,128]{3,1,2,0:T(8,128)S(1)} fusion(f32[4,16,16,128]{3,1,2,0:T(8,128)S(1)} %get-tuple-element.1038, s32[]{:T(128)} %get-tuple-element.1037, f32[16,16,8,128]{3,0,2,1:T(8,128)S(1)} %bitcast.398, f32[16,8,128]{2,1,0:T(8,128)S(1)} %bitcast.431, f32[16,128]{1,0:T(8,128)S(1)} %bitcast.443, f32[16,8,128]{2,1,0:T(8,128)S(1)} %bitcast.430, ...), kind=kOutput, calls=%fused_computation.87.clone.1 | convolution fusion | flops 432013312 | bytes 1327108 | tf_op jit(solution)/shard_map/while/body/eval_jaxpr/rjab,drjb->dra/dot_general | solution.py:61
  179.2 12.2 %fusion.501 = f32[4,16,16,128]{3,1,2,0:T(8,128)S(1)} fusion(f32[4,16,16,128]{3,1,2,0:T(8,128)S(1)} %get-tuple-element.1038, s32[]{:T(128)} %get-tuple-element.1037, f32[16,16,8,128]{3,0,2,1:T(8,128)S(1)} %bitcast.398, f32[16,8,128]{2,1,0:T(8,128)S(1)} %bitcast.431, f32[16,128]{1,0:T(8,128)S(1)} %bitcast.443, f32[16,8,128]{2,1,0:T(8,128)S(1)} %bitcast.430, ...), kind=kOutput, calls=%fused_computation.87.clone.1 | convolution fusion | flops 432013312 | bytes 1327108 | tf_op jit(solution)/shard_map/while/body/eval_jaxpr/rjab,drjb->dra/dot_general | solution.py:61
  195.7 12.2 %fusion.501 = f32[4,16,16,128]{3,1,2,0:T(8,128)S(1)} fusion(f32[4,16,16,128]{3,1,2,0:T(8,128)S(1)} %get-tuple-element.1038, s32[]{:T(128)} %get-tuple-element.1037, f32[16,16,8,128]{3,0,2,1:T(8,128)S(1)} %bitcast.398, f32[16,8,128]{2,1,0:T(8,128)S(1)} %bitcast.431, f32[16,128]{1,0:T(8,128)S(1)} %bitcast.443, f32[16,8,128]{2,1,0:T(8,128)S(1)} %bitcast.430, ...), kind=kOutput, calls=%fused_computation.87.clone.1 | convolution fusion | flops 432013312 | bytes 1327108 | tf_op jit(solution)/shard_map/while/body/eval_jaxpr/rjab,drjb->dra/dot_general | solution.py:61
  208.7 15.4 %all_to_all.205 = f32[16,8,1024]{2,0,1:T(8,128)S(1)} all-to-all(f32[16,8,1024]{2,0,1:T(8,128)S(1)} %copy.124), channel_id=1, replica_groups=mesh['space'=8,'tm'=16] {'space'}, dimensions={1} | all-to-all | bytes 1048576 | tf_op jit(solution)/shard_map/all_to_all | solution.py:73
  242.8 8.6 all-to-all-done.4
  252.1 66.4 %while.74 = (s32[]{:T(128)}, f32[4,16,16,128]{3,1,2,0:T(8,128)S(1)}, s32[4]{0:T(128)S(1)}, s32[64,8]{1,0:T(8,128)S(1)}, f32[16,64,128]{2,0,1:T(8,128)S(1)}, /*index=5*/f32[2,64,128]{2,0,1:T(2,128)S(1)}, s32[]{:T(128)}) while((s32[]{:T(128)}, f32[4,16,16,128]{3,1,2,0:T(8,128)S(1)}, s32[4]{0:T(128)S(1)}, s32[64,8]{1,0:T(8,128)S(1)}, ...), condition=%wide.region_7.8_spmd, body=%wide.region_6.7_spmd.sunk | while | flops 432015808 | bytes 4029281 | solution.py:64
  256.5 12.2 %fusion.507 = f32[4,16,16,128]{3,1,2,0:T(8,128)S(1)} fusion(f32[4,16,16,128]{3,1,2,0:T(8,128)S(1)} %get-tuple-element.1059, s32[]{:T(128)} %get-tuple-element.1058, f32[16,16,8,128]{3,0,2,1:T(8,128)S(1)} %bitcast.399, f32[16,8,128]{2,1,0:T(8,128)S(1)} %bitcast.433, f32[16,128]{1,0:T(8,128)S(1)} %bitcast.445, f32[16,8,128]{2,1,0:T(8,128)S(1)} %bitcast.432, ...), kind=kOutput, calls=%fused_computation.124.clone.1 | convolution fusion | flops 432013312 | bytes 1327108 | tf_op jit(solution)/shard_map/while/body/eval_jaxpr/rjab,drjb->dra/dot_general | solution.py:61
  273.0 12.2 %fusion.507 = f32[4,16,16,128]{3,1,2,0:T(8,128)S(1)} fusion(f32[4,16,16,128]{3,1,2,0:T(8,128)S(1)} %get-tuple-element.1059, s32[]{:T(128)} %get-tuple-element.1058, f32[16,16,8,128]{3,0,2,1:T(8,128)S(1)} %bitcast.399, f32[16,8,128]{2,1,0:T(8,128)S(1)} %bitcast.433, f32[16,128]{1,0:T(8,128)S(1)} %bitcast.445, f32[16,8,128]{2,1,0:T(8,128)S(1)} %bitcast.432, ...), kind=kOutput, calls=%fused_computation.124.clone.1 | convolution fusion | flops 432013312 | bytes 1327108 | tf_op jit(solution)/shard_map/while/body/eval_jaxpr/rjab,drjb->dra/dot_general | solution.py:61
  289.5 12.2 %fusion.507 = f32[4,16,16,128]{3,1,2,0:T(8,128)S(1)} fusion(f32[4,16,16,128]{3,1,2,0:T(8,128)S(1)} %get-tuple-element.1059, s32[]{:T(128)} %get-tuple-element.1058, f32[16,16,8,128]{3,0,2,1:T(8,128)S(1)} %bitcast.399, f32[16,8,128]{2,1,0:T(8,128)S(1)} %bitcast.433, f32[16,128]{1,0:T(8,128)S(1)} %bitcast.445, f32[16,8,128]{2,1,0:T(8,128)S(1)} %bitcast.432, ...), kind=kOutput, calls=%fused_computation.124.clone.1 | convolution fusion | flops 432013312 | bytes 1327108 | tf_op jit(solution)/shard_map/while/body/eval_jaxpr/rjab,drjb->dra/dot_general | solution.py:61
  305.9 12.2 %fusion.507 = f32[4,16,16,128]{3,1,2,0:T(8,128)S(1)} fusion(f32[4,16,16,128]{3,1,2,0:T(8,128)S(1)} %get-tuple-element.1059, s32[]{:T(128)} %get-tuple-element.1058, f32[16,16,8,128]{3,0,2,1:T(8,128)S(1)} %bitcast.399, f32[16,8,128]{2,1,0:T(8,128)S(1)} %bitcast.433, f32[16,128]{1,0:T(8,128)S(1)} %bitcast.445, f32[16,8,128]{2,1,0:T(8,128)S(1)} %bitcast.432, ...), kind=kOutput, calls=%fused_computation.124.clone.1 | convolution fusion | flops 432013312 | bytes 1327108 | tf_op jit(solution)/shard_map/while/body/eval_jaxpr/rjab,drjb->dra/dot_general | solution.py:61
  319.1 15.4 %all_to_all.206 = f32[16,8,1024]{2,0,1:T(8,128)S(1)} all-to-all(f32[16,8,1024]{2,0,1:T(8,128)S(1)} %copy.129), channel_id=1, replica_groups=mesh['space'=8,'tm'=16] {'space'}, dimensions={1} | all-to-all | bytes 1048576 | tf_op jit(solution)/shard_map/all_to_all | solution.py:73
  351.9 8.6 all-to-all-done.6
  361.2 66.0 %while.75 = (s32[]{:T(128)}, f32[4,16,16,128]{3,1,2,0:T(8,128)S(1)}, s32[4]{0:T(128)S(1)}, s32[64,8]{1,0:T(8,128)S(1)}, f32[16,64,128]{2,0,1:T(8,128)S(1)}, /*index=5*/f32[2,64,128]{2,0,1:T(2,128)S(1)}, s32[]{:T(128)}) while((s32[]{:T(128)}, f32[4,16,16,128]{3,1,2,0:T(8,128)S(1)}, s32[4]{0:T(128)S(1)}, s32[64,8]{1,0:T(8,128)S(1)}, ...), condition=%wide.region_9.10_spmd, body=%wide.region_8.9_spmd.sunk | while | flops 432015808 | bytes 4029281 | solution.py:64
  365.6 12.2 %fusion.513 = f32[4,16,16,128]{3,1,2,0:T(8,128)S(1)} fusion(f32[4,16,16,128]{3,1,2,0:T(8,128)S(1)} %get-tuple-element.1080, s32[]{:T(128)} %get-tuple-element.1079, f32[16,16,8,128]{3,0,2,1:T(8,128)S(1)} %bitcast.400, f32[16,8,128]{2,1,0:T(8,128)S(1)} %bitcast.435, f32[16,128]{1,0:T(8,128)S(1)} %bitcast.447, f32[16,8,128]{2,1,0:T(8,128)S(1)} %bitcast.434, ...), kind=kOutput, calls=%fused_computation.161.clone.1 | convolution fusion | flops 432013312 | bytes 1327108 | tf_op jit(solution)/shard_map/while/body/eval_jaxpr/rjab,drjb->dra/dot_general | solution.py:61
  382.1 12.2 %fusion.513 = f32[4,16,16,128]{3,1,2,0:T(8,128)S(1)} fusion(f32[4,16,16,128]{3,1,2,0:T(8,128)S(1)} %get-tuple-element.1080, s32[]{:T(128)} %get-tuple-element.1079, f32[16,16,8,128]{3,0,2,1:T(8,128)S(1)} %bitcast.400, f32[16,8,128]{2,1,0:T(8,128)S(1)} %bitcast.435, f32[16,128]{1,0:T(8,128)S(1)} %bitcast.447, f32[16,8,128]{2,1,0:T(8,128)S(1)} %bitcast.434, ...), kind=kOutput, calls=%fused_computation.161.clone.1 | convolution fusion | flops 432013312 | bytes 1327108 | tf_op jit(solution)/shard_map/while/body/eval_jaxpr/rjab,drjb->dra/dot_general | solution.py:61
  398.6 12.2 %fusion.513 = f32[4,16,16,128]{3,1,2,0:T(8,128)S(1)} fusion(f32[4,16,16,128]{3,1,2,0:T(8,128)S(1)} %get-tuple-element.1080, s32[]{:T(128)} %get-tuple-element.1079, f32[16,16,8,128]{3,0,2,1:T(8,128)S(1)} %bitcast.400, f32[16,8,128]{2,1,0:T(8,128)S(1)} %bitcast.435, f32[16,128]{1,0:T(8,128)S(1)} %bitcast.447, f32[16,8,128]{2,1,0:T(8,128)S(1)} %bitcast.434, ...), kind=kOutput, calls=%fused_computation.161.clone.1 | convolution fusion | flops 432013312 | bytes 1327108 | tf_op jit(solution)/shard_map/while/body/eval_jaxpr/rjab,drjb->dra/dot_general | solution.py:61
  415.1 12.2 %fusion.513 = f32[4,16,16,128]{3,1,2,0:T(8,128)S(1)} fusion(f32[4,16,16,128]{3,1,2,0:T(8,128)S(1)} %get-tuple-element.1080, s32[]{:T(128)} %get-tuple-element.1079, f32[16,16,8,128]{3,0,2,1:T(8,128)S(1)} %bitcast.400, f32[16,8,128]{2,1,0:T(8,128)S(1)} %bitcast.435, f32[16,128]{1,0:T(8,128)S(1)} %bitcast.447, f32[16,8,128]{2,1,0:T(8,128)S(1)} %bitcast.434, ...), kind=kOutput, calls=%fused_computation.161.clone.1 | convolution fusion | flops 432013312 | bytes 1327108 | tf_op jit(solution)/shard_map/while/body/eval_jaxpr/rjab,drjb->dra/dot_general | solution.py:61
  427.8 15.4 %all_to_all.207 = f32[16,8,1024]{2,0,1:T(8,128)S(1)} all-to-all(f32[16,8,1024]{2,0,1:T(8,128)S(1)} %copy.134), channel_id=1, replica_groups=mesh['space'=8,'tm'=16] {'space'}, dimensions={1} | all-to-all | bytes 1048576 | tf_op jit(solution)/shard_map/all_to_all | solution.py:73
  444.0 65.9 %all-reduce = (f32[]{:T(128)}, f32[]{:T(128)}) all-reduce(f32[]{:T(128)} %get-tuple-element.714, f32[]{:T(128)} %multiply_reduce_fusion.2), channel_id=1, replica_groups=mesh['space'=8,'tm'=16] {'space','tm'}, use_global_device_ids=true, to_apply=%region_5.6 | all-reduce | flops 2 | bytes 16 | tf_op jit(solution)/shard_map/psum | solution.py:77
  512.0 62.3 %psum.30 = f32[]{:T(128)} all-reduce(f32[]{:T(128)} %multiply_reduce_fusion.1), channel_id=1, replica_groups=mesh['space'=8,'tm'=16] {'space','tm'}, use_global_device_ids=true, to_apply=%region_13.14 | all-reduce | flops 1 | bytes 8 | tf_op jit(solution)/shard_map/psum | solution.py:77
  581.8 7.1 fusion.262
  592.4 8.6 all-to-all-done.8
  602.5 69.0 %while.76 = (s32[]{:T(128)}, f32[4,16,16,128]{3,1,2,0:T(8,128)}, s32[4]{0:T(128)S(1)}, s32[64,8]{1,0:T(8,128)S(1)}, f32[16,64,128]{2,0,1:T(8,128)S(1)}, /*index=5*/f32[2,64,128]{2,0,1:T(2,128)S(1)}, s32[]{:T(128)}) while((s32[]{:T(128)}, f32[4,16,16,128]{3,1,2,0:T(8,128)}, s32[4]{0:T(128)S(1)}, s32[64,8]{1,0:T(8,128)S(1)}, ...), condition=%wide.region_15.16_spmd, body=%wide.region_14.15_spmd.sunk | while | flops 432015808 | bytes 4029789 | solution.py:64
  607.0 12.8 %fusion.519 = f32[4,16,16,128]{3,1,2,0:T(8,128)} fusion(f32[4,16,16,128]{3,1,2,0:T(8,128)} %get-tuple-element.1101, s32[]{:T(128)} %get-tuple-element.1100, f32[16,16,8,128]{3,0,2,1:T(8,128)S(1)} %bitcast.401, f32[16,8,128]{2,1,0:T(8,128)S(1)} %bitcast.437, f32[16,128]{1,0:T(8,128)S(1)} %bitcast.449, f32[16,8,128]{2,1,0:T(8,128)S(1)} %bitcast.436, ...), kind=kOutput, calls=%fused_computation.198.clone.1 | convolution fusion | flops 432013312 | bytes 1327616 | tf_op jit(solution)/shard_map/while/body/eval_jaxpr/rjab,drjb->dra/dot_general | solution.py:61
  624.2 12.8 %fusion.519 = f32[4,16,16,128]{3,1,2,0:T(8,128)} fusion(f32[4,16,16,128]{3,1,2,0:T(8,128)} %get-tuple-element.1101, s32[]{:T(128)} %get-tuple-element.1100, f32[16,16,8,128]{3,0,2,1:T(8,128)S(1)} %bitcast.401, f32[16,8,128]{2,1,0:T(8,128)S(1)} %bitcast.437, f32[16,128]{1,0:T(8,128)S(1)} %bitcast.449, f32[16,8,128]{2,1,0:T(8,128)S(1)} %bitcast.436, ...), kind=kOutput, calls=%fused_computation.198.clone.1 | convolution fusion | flops 432013312 | bytes 1327616 | tf_op jit(solution)/shard_map/while/body/eval_jaxpr/rjab,drjb->dra/dot_general | solution.py:61
  641.4 12.8 %fusion.519 = f32[4,16,16,128]{3,1,2,0:T(8,128)} fusion(f32[4,16,16,128]{3,1,2,0:T(8,128)} %get-tuple-element.1101, s32[]{:T(128)} %get-tuple-element.1100, f32[16,16,8,128]{3,0,2,1:T(8,128)S(1)} %bitcast.401, f32[16,8,128]{2,1,0:T(8,128)S(1)} %bitcast.437, f32[16,128]{1,0:T(8,128)S(1)} %bitcast.449, f32[16,8,128]{2,1,0:T(8,128)S(1)} %bitcast.436, ...), kind=kOutput, calls=%fused_computation.198.clone.1 | convolution fusion | flops 432013312 | bytes 1327616 | tf_op jit(solution)/shard_map/while/body/eval_jaxpr/rjab,drjb->dra/dot_general | solution.py:61
  658.6 12.8 %fusion.519 = f32[4,16,16,128]{3,1,2,0:T(8,128)} fusion(f32[4,16,16,128]{3,1,2,0:T(8,128)} %get-tuple-element.1101, s32[]{:T(128)} %get-tuple-element.1100, f32[16,16,8,128]{3,0,2,1:T(8,128)S(1)} %bitcast.401, f32[16,8,128]{2,1,0:T(8,128)S(1)} %bitcast.437, f32[16,128]{1,0:T(8,128)S(1)} %bitcast.449, f32[16,8,128]{2,1,0:T(8,128)S(1)} %bitcast.436, ...), kind=kOutput, calls=%fused_computation.198.clone.1 | convolution fusion | flops 432013312 | bytes 1327616 | tf_op jit(solution)/shard_map/while/body/eval_jaxpr/rjab,drjb->dra/dot_general | solution.py:61
  673.1 15.4 %all_to_all.208 = f32[16,8,1024]{2,0,1:T(8,128)S(1)} all-to-all(f32[16,8,1024]{2,0,1:T(8,128)S(1)} %copy.139), channel_id=1, replica_groups=mesh['space'=8,'tm'=16] {'space'}, dimensions={1} | all-to-all | bytes 1048576 | tf_op jit(solution)/shard_map/all_to_all | solution.py:73
  701.3 12.2 %all_to_all.209 = f32[8,16,1024]{2,1,0:T(8,128)S(1)} all-to-all(f32[8,16,1024]{2,1,0:T(8,128)S(1)} %bitcast.410), channel_id=1, replica_groups=mesh['space'=8,'tm'=16] {'space'}, dimensions={0} | all-to-all | bytes 1048576 | tf_op jit(solution)/shard_map/all_to_all | solution.py:69
  715.1 68.8 %while.77 = (s32[]{:T(128)}, f32[4,16,16,128]{3,1,2,0:T(8,128)}, s32[4]{0:T(128)S(1)}, s32[64,8]{1,0:T(8,128)S(1)}, f32[16,64,128]{2,0,1:T(8,128)S(1)}, /*index=5*/f32[2,64,128]{2,0,1:T(2,128)S(1)}, s32[]{:T(128)}) while((s32[]{:T(128)}, f32[4,16,16,128]{3,1,2,0:T(8,128)}, s32[4]{0:T(128)S(1)}, s32[64,8]{1,0:T(8,128)S(1)}, ...), condition=%wide.region_17.18_spmd, body=%wide.region_16.17_spmd.sunk | while | flops 432015808 | bytes 4029789 | solution.py:64
  719.6 12.8 %fusion.525 = f32[4,16,16,128]{3,1,2,0:T(8,128)} fusion(f32[4,16,16,128]{3,1,2,0:T(8,128)} %get-tuple-element.1122, s32[]{:T(128)} %get-tuple-element.1121, f32[16,16,8,128]{3,0,2,1:T(8,128)S(1)} %bitcast.402, f32[16,8,128]{2,1,0:T(8,128)S(1)} %bitcast.439, f32[16,128]{1,0:T(8,128)S(1)} %bitcast.451, f32[16,8,128]{2,1,0:T(8,128)S(1)} %bitcast.438, ...), kind=kOutput, calls=%fused_computation.235.clone.1 | convolution fusion | flops 432013312 | bytes 1327616 | tf_op jit(solution)/shard_map/while/body/eval_jaxpr/rjab,drjb->dra/dot_general | solution.py:61
  736.7 12.8 %fusion.525 = f32[4,16,16,128]{3,1,2,0:T(8,128)} fusion(f32[4,16,16,128]{3,1,2,0:T(8,128)} %get-tuple-element.1122, s32[]{:T(128)} %get-tuple-element.1121, f32[16,16,8,128]{3,0,2,1:T(8,128)S(1)} %bitcast.402, f32[16,8,128]{2,1,0:T(8,128)S(1)} %bitcast.439, f32[16,128]{1,0:T(8,128)S(1)} %bitcast.451, f32[16,8,128]{2,1,0:T(8,128)S(1)} %bitcast.438, ...), kind=kOutput, calls=%fused_computation.235.clone.1 | convolution fusion | flops 432013312 | bytes 1327616 | tf_op jit(solution)/shard_map/while/body/eval_jaxpr/rjab,drjb->dra/dot_general | solution.py:61
  753.9 12.8 %fusion.525 = f32[4,16,16,128]{3,1,2,0:T(8,128)} fusion(f32[4,16,16,128]{3,1,2,0:T(8,128)} %get-tuple-element.1122, s32[]{:T(128)} %get-tuple-element.1121, f32[16,16,8,128]{3,0,2,1:T(8,128)S(1)} %bitcast.402, f32[16,8,128]{2,1,0:T(8,128)S(1)} %bitcast.439, f32[16,128]{1,0:T(8,128)S(1)} %bitcast.451, f32[16,8,128]{2,1,0:T(8,128)S(1)} %bitcast.438, ...), kind=kOutput, calls=%fused_computation.235.clone.1 | convolution fusion | flops 432013312 | bytes 1327616 | tf_op jit(solution)/shard_map/while/body/eval_jaxpr/rjab,drjb->dra/dot_general | solution.py:61
  771.0 12.8 %fusion.525 = f32[4,16,16,128]{3,1,2,0:T(8,128)} fusion(f32[4,16,16,128]{3,1,2,0:T(8,128)} %get-tuple-element.1122, s32[]{:T(128)} %get-tuple-element.1121, f32[16,16,8,128]{3,0,2,1:T(8,128)S(1)} %bitcast.402, f32[16,8,128]{2,1,0:T(8,128)S(1)} %bitcast.439, f32[16,128]{1,0:T(8,128)S(1)} %bitcast.451, f32[16,8,128]{2,1,0:T(8,128)S(1)} %bitcast.438, ...), kind=kOutput, calls=%fused_computation.235.clone.1 | convolution fusion | flops 432013312 | bytes 1327616 | tf_op jit(solution)/shard_map/while/body/eval_jaxpr/rjab,drjb->dra/dot_general | solution.py:61
  785.5 13.7 %all_to_all.210 = f32[16,8,1024]{2,0,1:T(8,128)S(1)} all-to-all(f32[16,8,1024]{2,0,1:T(8,128)S(1)} %copy.144), channel_id=1, replica_groups=mesh['space'=8,'tm'=16] {'space'}, dimensions={1} | all-to-all | bytes 1048576 | tf_op jit(solution)/shard_map/all_to_all | solution.py:73
  800.0 65.8 %psum.31 = f32[]{:T(128)} all-reduce(f32[]{:T(128)} %multiply_reduce_fusion), channel_id=1, replica_groups=mesh['space'=8,'tm'=16] {'space','tm'}, use_global_device_ids=true, to_apply=%region_19.20 | all-reduce | flops 1 | bytes 8 | tf_op jit(solution)/shard_map/psum | solution.py:100
  (444 shorter events, 201.3 us)
Async XLA Ops:
  0.6 7.1 copy-start.3
  1.5 4.2 collective-permute-start
  2.8 4.9 collective-permute-start.1
  15.0 6.5 copy-start.5
  15.0 15.3 %all-to-all-start = ((f32[8,16,1024]{2,1,0:T(8,128)}), f32[8,16,1024]{2,1,0:T(8,128)S(1)}, u32[]{:S(2)}, u32[]{:S(2)}) async-start(f32[8,16,1024]{2,1,0:T(8,128)} %bitcast.111), calls=%async_computation | async-start | bytes 1048576 | tf_op jit(solution)/shard_map/all_to_all | solution.py:69
  30.7 0.8 copy-start
  98.6 15.7 %copy-start.4 = (s32[128,1024]{1,0:T(8,128)S(1)}, s32[128,1024]{1,0:T(8,128)}, u32[]{:S(2)}) copy-start(s32[128,1024]{1,0:T(8,128)} %param.18) | copy-start | bytes 1572868
  114.3 220.2 %copy-start.1 = (f32[16,8,1024]{2,0,1:T(8,128)}, f32[16,8,1024]{2,0,1:T(8,128)S(1)}, u32[]{:S(2)}) copy-start(f32[16,8,1024]{2,0,1:T(8,128)S(1)} %exp.9) | copy-start | bytes 1572868
  114.4 2.6 collective-permute-start.2
  115.7 6.3 collective-permute-start.3
  129.1 12.1 %all-to-all-start.2 = ((f32[8,16,1024]{2,1,0:T(8,128)}), f32[8,16,1024]{2,1,0:T(8,128)S(1)}, u32[]{:S(2)}, u32[]{:S(2)}) async-start(f32[8,16,1024]{2,1,0:T(8,128)} %bitcast.117), calls=%async_computation.2 | async-start | bytes 1048576 | tf_op jit(solution)/shard_map/all_to_all | solution.py:69
  224.8 2.6 collective-permute-start.4
  226.1 6.1 collective-permute-start.5
  239.3 12.1 %all-to-all-start.4 = ((f32[8,16,1024]{2,1,0:T(8,128)}), f32[8,16,1024]{2,1,0:T(8,128)S(1)}, u32[]{:S(2)}, u32[]{:S(2)}) async-start(f32[8,16,1024]{2,1,0:T(8,128)} %bitcast.123), calls=%async_computation.4 | async-start | bytes 1048576 | tf_op jit(solution)/shard_map/all_to_all | solution.py:69
  334.6 2.6 collective-permute-start.6
  335.9 5.4 collective-permute-start.7
  348.4 12.1 %all-to-all-start.6 = ((f32[8,16,1024]{2,1,0:T(8,128)}), f32[8,16,1024]{2,1,0:T(8,128)S(1)}, u32[]{:S(2)}, u32[]{:S(2)}) async-start(f32[8,16,1024]{2,1,0:T(8,128)} %bitcast.128), calls=%async_computation.6 | async-start | bytes 1048576 | tf_op jit(solution)/shard_map/all_to_all | solution.py:69
  575.6 3.2 collective-permute-start.8
  577.5 4.3 collective-permute-start.9
  588.9 12.1 %all-to-all-start.8 = ((f32[8,16,1024]{2,1,0:T(8,128)}), f32[8,16,1024]{2,1,0:T(8,128)S(1)}, u32[]{:S(2)}, u32[]{:S(2)}) async-start(f32[8,16,1024]{2,1,0:T(8,128)} %bitcast.133), calls=%async_computation.8 | async-start | bytes 1048576 | tf_op jit(solution)/shard_map/all_to_all | solution.py:69
  672.8 15.7 %copy-start.2 = (f32[16,8,1024]{2,0,1:T(8,128)S(1)}, f32[16,8,1024]{2,0,1:T(8,128)}, u32[]{:S(2)}) copy-start(f32[16,8,1024]{2,0,1:T(8,128)} %copy-done.1) | copy-start | bytes 1572868
  688.6 2.6 collective-permute-start.10
  689.9 5.1 collective-permute-start.11
where the time goes:
time: 873 us; the launch traced here: 868 us
  matrix products  297 us (34%)
  blocking collectives  297 us (34%)
  local copies, waits for them, and re-layouts  102 us (12%)
  waiting for transfers between devices  64.3 us (7%)
  other arithmetic  62.5 us (7%)
  starting transfers between devices  36.5 us (4%)
    dot_general x24, matrix products, group_out(): jnp.einsum('rjab,drjb->dra', weight, picked, precision=lax.Precision.HIGH...  297 us
    psum x2, blocking collectives, residual_norm(): return lax.psum(jnp.sum(residual * residual), ('space', 'tm'))  128 us
    all_to_all x6, blocking collectives, to_cells(): lax.all_to_all(field, 'space', split_axis=1, concat_axis=0, tiled=True)  90.9 us
    psum x1, blocking collectives, shards(): curvature = lax.psum(jnp.sum(direction * curved), ('space', 'tm'))  65.8 us
    all_to_all x5, waiting for transfers between devices, to_days(): lax.all_to_all(field, 'space', split_axis=0, concat_axis=1, tiled=True)  42.9 us
    add x6, other arithmetic, band_product(): summed + temporal_taps[offset] * (padded[BW - offset:BW - offset + length...  42.1 us
    ppermute x6, waiting for transfers between devices, with_halo(): lax.ppermute(lax.slice_in_dim(block, 0, width, axis=dim), axis, backward)  21.4 us
    all_to_all x5, starting transfers between devices, to_days(): lax.all_to_all(field, 'space', split_axis=0, concat_axis=1, tiled=True)  20.4 us
  transfers between devices with their start and end apart: 17, of which 11 were waited for; matrix products, arithmetic and copies ran while one was open for 0% of the time, Pallas kernels for 0%

commit v1 on v0

v1 whole, which is shorter than its diff:
```python
import jax
import jax.numpy as jnp
from jax import lax
from jax.sharding import PartitionSpec as P

BLOCK = 128
BW = 8
ITERS = 2


support = 0.25
amplitude = 0.2


def wendland(distance):
    scaled = distance / support
    remain = jnp.maximum(1.0 - scaled, 0.0)
    return amplitude * remain**4 * (1.0 + 4.0 * scaled)


def spatial_weights(coords, pattern):
    blocks = pattern.shape[0]
    located = coords.reshape(2, blocks, BLOCK)
    row_coords = located[:, :, None, None, :]
    col_coords = located[:, pattern][:, :, :, :, None]
    delta_x = row_coords[0] - col_coords[0]
    delta_y = row_coords[1] - col_coords[1]
    weight = wendland(jnp.sqrt(delta_x * delta_x + delta_y * delta_y))
    return weight.reshape(blocks, pattern.shape[1] * BLOCK, BLOCK)


def day_order_halo(field):
    spaces, times = lax.axis_size("space"), lax.axis_size("tm")
    place = [(rank % spaces) * times + rank // spaces for rank in range(spaces * times)]
    forward = [(place[i], place[i + 1]) for i in range(len(place) - 1)]
    backward = [(place[i + 1], place[i]) for i in range(len(place) - 1)]
    axes = ("space", "tm")
    low = lax.ppermute(field[field.shape[0] - BW :], axes, forward)
    high = lax.ppermute(field[:BW], axes, backward)
    return jnp.concatenate([low, field, high], axis=0)


def band_product(field, temporal_taps):
    length = field.shape[0]
    padded = day_order_halo(field)
    summed = temporal_taps[0] * field
    for offset in range(1, BW + 1):
        summed = summed + temporal_taps[offset] * (
            padded[BW - offset : BW - offset + length] + padded[BW + offset : BW + offset + length]
        )
    return summed


def block_product(field, weights, pattern):
    day_count = field.shape[0]
    blocks = pattern.shape[0]
    blocked = field.reshape(day_count, blocks, BLOCK)
    picked = blocked[:, pattern].reshape(day_count, blocks, pattern.shape[1] * BLOCK)
    out = jnp.einsum("rkc,drk->drc", weights, picked, precision=lax.Precision.HIGH)
    return out.reshape(day_count, blocks * BLOCK)


def to_days(field):
    return lax.all_to_all(field, "space", split_axis=1, concat_axis=2, tiled=True)


def to_cells(field):
    return lax.all_to_all(field, "space", split_axis=2, concat_axis=1, tiled=True)


def total(values):
    v = jnp.broadcast_to(jnp.stack(values)[:, None], (len(values), 128))
    for axis in ("space", "tm"):
        n = lax.axis_size(axis)
        k = 1
        while k < n:
            v = v + lax.ppermute(v, axis, [(i, i ^ k) for i in range(n)])
            k *= 2
    return [v[i, 0] for i in range(len(values))]


def shards(coefficients, counts, coords, pattern, temporal_taps):
    weights = spatial_weights(coords, pattern)

    def spread(field):
        return block_product(band_product(field, temporal_taps), weights, pattern)

    both = to_days(jnp.stack([coefficients, counts.astype(jnp.float32)]))
    coef, cnt = both[0], both[1]
    latent = spread(coef)
    intensity = jnp.exp(latent)
    gradient = coef + spread(intensity - cnt)
    residual = -gradient
    direction = residual
    newton_step = jnp.zeros_like(residual)
    norm_part = jnp.sum(residual * residual)
    norm_now = None
    for iteration in range(ITERS):
        image = spread(direction)
        weighted = intensity * image
        curv_part = jnp.sum(direction * direction) + jnp.sum(weighted * image)
        if norm_now is None:
            norm_now, curvature = total([norm_part, curv_part])
        else:
            (curvature,) = total([curv_part])
        curved = direction + spread(weighted)
        step_size = norm_now / curvature
        newton_step = newton_step + step_size * direction
        residual = residual - step_size * curved
        if iteration + 1 < ITERS:
            (norm_next,) = total([jnp.sum(residual * residual)])
            direction = residual + norm_next / norm_now * direction
            norm_now = norm_next
    out = to_cells(jnp.stack([newton_step, residual]))
    return (out[0], out[1])


def solution(mesh):
    placed = (P("tm", "space"), P("tm", "space"), P(), P(), P())
    return jax.shard_map(
        shards,
        mesh=mesh,
        in_specs=placed,
        out_specs=(P("tm", "space"), P("tm", "space")),
        check_vma=False,
    )
```

time: 873 us -> 605 us (0.69)
  blocking collectives: 297 us -> 15.7 us
  starting transfers between devices: 36.5 us -> 82 us
  local copies, waits for them, and re-layouts: 102 us -> 77.5 us
  matrix products: 297 us -> 273 us
  waiting for transfers between devices: 64.3 us -> 77.7 us
    psum x3 -> x0, blocking collectives: 194 us -> none  [the longest x2 128 us: residual_norm(): return lax.psum(jnp.sum(residual * residual), ('space', 'tm'))]
    all_to_all x7 -> x1, blocking collectives: 103 us -> 15.7 us  [to_cells(): lax.all_to_all(field, 'space', split_axis=2, concat_axis=1, tiled=True)]
    ppermute x12 -> x33, starting transfers between devices: 16.1 us -> 75.6 us  [the longest x21 46 us: total(): v = v + lax.ppermute(v, axis, [(i, i ^ k) for i in range(n)])]
    ppermute x12 -> x33, waiting for transfers between devices: 21.4 us -> 70 us  [the longest x21 44.5 us: total(): v = v + lax.ppermute(v, axis, [(i, i ^ k) for i in range(n)])]
    reshape x0 -> x6, other arithmetic: none -> 46.5 us  [block_product(): blocked = field.reshape(day_count, blocks, BLOCK)]
    gather x120 -> x7, local copies, waits for them, and re-layouts: 65.3 us -> 20.9 us  [the longest x6 18.6 us: block_product(): blocked[:, pattern].reshape(day_count, blocks, pattern.shape[1] * BLOCK)]
    add x6 -> x22, other arithmetic: 42.1 us -> 1.82 us  [the longest x21 1.57 us: total(): v = v + lax.ppermute(v, axis, [(i, i ^ k) for i in range(n)])]
    all_to_all x5 -> x1, waiting for transfers between devices: 42.9 us -> 7.77 us  [to_days(): lax.all_to_all(field, 'space', split_axis=1, concat_axis=2, tiled=True)]
  transfers between devices with their start and end apart: 17 -> 34, of which waited for: 11 -> 27; matrix products, arithmetic and copies ran while one was open for 0% -> 2% of each run, Pallas kernels for 0% -> 0%
where the time goes in v1:
time: 605 us; the launch traced here: 596 us
  matrix products  273 us (45%)
  starting transfers between devices  82 us (14%)
  waiting for transfers between devices  77.7 us (13%)
  local copies, waits for them, and re-layouts  77.5 us (13%)
  other arithmetic  63.7 us (11%)
  blocking collectives  15.7 us (3%)
    dot_general x6, matrix products, block_product(): jnp.einsum('rkc,drk->drc', weights, picked, precision=lax.Precision.HIGH)  273 us
    reshape x6, other arithmetic, block_product(): blocked = field.reshape(day_count, blocks, BLOCK)  46.5 us
    ppermute x21, starting transfers between devices, total(): v = v + lax.ppermute(v, axis, [(i, i ^ k) for i in range(n)])  46 us
    ppermute x21, waiting for transfers between devices, total(): v = v + lax.ppermute(v, axis, [(i, i ^ k) for i in range(n)])  44.5 us
    unnamed x21, local copies, waits for them, and re-layouts  28 us
    ppermute x6, starting transfers between devices, day_order_halo(): low = lax.ppermute(field[field.shape[0] - BW:], axes, forward)  21.3 us
    gather x6, local copies, waits for them, and re-layouts, block_product(): blocked[:, pattern].reshape(day_count, blocks, pattern.shape[1] * BLOCK)  18.6 us
    ppermute x6, waiting for transfers between devices, day_order_halo(): high = lax.ppermute(field[:BW], axes, backward)  18.6 us
  transfers between devices with their start and end apart: 34, of which 27 were waited for; matrix products, arithmetic and copies ran while one was open for 2% of the time, Pallas kernels for 0%

profile of v1, /device:TPU:0, one launch (start us, length us, event | category | flops | bytes accessed | tf_op | source)
XLA Modules:
  0.0 595.9 jit_solution(1717425539891031414)
XLA Ops:
  5.4 6.4 %all-to-all-start = ((f32[2,128,1024]{2,0,1:T(2,128)}), f32[2,128,1024]{2,0,1:T(2,128)S(1)}, u32[]{:S(2)}, u32[]{:S(2)}) async-start(f32[2,128,1024]{2,0,1:T(2,128)} %pad_maximum_fusion), calls=%async_computation | async-start | bytes 2097152 | tf_op jit(solution)/shard_map/all_to_all | solution.py:64
  18.9 7.8 %all-to-all-done = f32[2,128,1024]{2,0,1:T(2,128)S(1)} async-done(((f32[2,128,1024]{2,0,1:T(2,128)}), f32[2,128,1024]{2,0,1:T(2,128)S(1)}, u32[]{:S(2)}, u32[]{:S(2)}) %all-to-all-start) | async-done | bytes 1048608 | tf_op jit(solution)/shard_map/all_to_all | solution.py:64
  31.3 3.4 collective-permute-done
  34.8 4.2 collective-permute-done.1
  39.0 6.5 %copy_bitcast_fusion.5 = f32[16,64,128]{2,0,1:T(8,128)S(1)} fusion(f32[24,8192]{1,0:T(8,128)S(1)} %constant_dynamic-update-slice_fusion.2, f32[24,8192]{1,0:T(8,128)S(1)} %get-tuple-element.24, f32[16,8192]{1,0:T(8,128)S(1)} %bitcast.195, f32[]{:T(128)} %bitcast.13, f32[]{:T(128)} %bitcast.12, f32[]{:T(128)} %bitcast.11, f32[]{:T(128)} %bitcast.10, ...), kind=kLoop, calls=%fused_computation.373 | loop fusion | flops 3276800 | bytes 9437220 | tf_op jit(solution)/shard_map/reshape | solution.py:57
  45.5 3.1 gather_fusion
  48.6 44.6 %fusion.18 = f32[64,16,128]{2,1,0:T(8,128)S(1)} fusion(f32[64,1024]{1,0:T(8,128)S(1)} %get-tuple-element.43, f32[64,128]{1,0:T(8,128)S(1)} %bitcast.224, f32[64,1024]{1,0:T(8,128)S(1)} %copy-done.6, f32[64,128]{1,0:T(8,128)S(1)} %bitcast.218, f32[64,8,2,8,128]{4,3,2,1,0:T(8,128)} %bitcast.200), kind=kOutput, calls=%fused_computation.166 | convolution fusion | flops 922746880 | bytes 5308416 | tf_op jit(solution)/shard_map/rkc,drk->drc/dot_general | solution.py:59
  97.1 3.1 collective-permute-done.2
  100.2 5.5 collective-permute-done.3
  105.7 6.9 %copy_bitcast_fusion.4 = f32[16,64,128]{2,0,1:T(8,128)S(1)} fusion(f32[16,8192]{1,0:T(8,128)S(1)} %bitcast_subtract_fusion, f32[8,8192]{1,0:T(8,128)S(1)} %collective-permute-done.3, f32[8,8192]{1,0:T(8,128)S(1)} %collective-permute-done.2, f32[]{:T(128)} %bitcast.13, f32[]{:T(128)} %bitcast.12, f32[]{:T(128)} %bitcast.11, f32[]{:T(128)} %bitcast.10, ...), kind=kLoop, calls=%fused_computation.372 | loop fusion | flops 5373952 | bytes 1572900 | tf_op jit(solution)/shard_map/reshape | solution.py:57
  112.6 3.1 gather_fusion.2
  115.7 45.1 %fusion.4 = f32[64,16,128]{2,1,0:T(8,128)S(1)} fusion(f32[64,1024]{1,0:T(8,128)S(1)} %get-tuple-element.43, f32[64,128]{1,0:T(8,128)S(1)} %bitcast.225, f32[64,1024]{1,0:T(8,128)} %get-tuple-element.44, f32[64,128]{1,0:T(8,128)S(1)} %bitcast.219, f32[64,8,2,8,128]{4,3,2,1,0:T(8,128)} %bitcast.203), kind=kOutput, calls=%fused_computation.12 | convolution fusion | flops 922746880 | bytes 5308416 | tf_op jit(solution)/shard_map/rkc,drk->drc/dot_general | solution.py:59
  161.7 6.2 %collective-permute-start.4 = (f32[8,8192]{1,0:T(8,128)}, f32[8,8192]{1,0:T(8,128)}, u32[]{:S(2)}, u32[]{:S(2)}) collective-permute-start(f32[8,8192]{1,0:T(8,128)} %get-tuple-element.20), channel_id=1, source_target_pairs={{0,16},{16,32},{32,48},{48,64},{64,80},{80,96},{96,112},{112,1},{1... | collective-permute-start | bytes 786440 | tf_op jit(solution)/shard_map/ppermute | solution.py:38
  171.4 5.1 collective-permute-done.5
  176.5 9.7 %copy_bitcast_fusion.3 = f32[16,64,128]{2,0,1:T(8,128)S(1)} fusion(f32[16,8192]{1,0:T(8,128)S(1)} %fusion.214, f32[8,8192]{1,0:T(8,128)} %collective-permute-done.5, f32[8,8192]{1,0:T(8,128)} %collective-permute-done.4, f32[]{:T(128)} %bitcast.13, f32[]{:T(128)} %bitcast.12, f32[]{:T(128)} %bitcast.11, f32[]{:T(128)} %bitcast.10, f32[]{:T(128)} %bitcast.9, ...), kind=kLoop, calls=%fused_computation.371 | loop fusion | flops 5373952 | bytes 1572900 | tf_op jit(solution)/shard_map/reshape | solution.py:57
  186.2 3.1 gather_fusion.3
  189.3 46.5 %fusion.24 = (f32[]{:T(128)}, f32[64,16,128]{2,1,0:T(8,128)S(1)}) fusion(f32[64,16,128]{2,1,0:T(8,128)S(1)} %fusion.18, f32[64,1024]{1,0:T(8,128)S(1)} %get-tuple-element.43, f32[64,128]{1,0:T(8,128)S(1)} %bitcast.226, f32[64,1024]{1,0:T(8,128)} %get-tuple-element.44, f32[64,128]{1,0:T(8,128)S(1)} %bitcast.220, f32[64,8,2,8,128]{4,3,2,1,0:T(8,128)} %bitcast.201), kind=kOutput, calls=%fused_computation.172 | convolution fusion | flops 923140096 | bytes 5832708 | tf_op jit(solution)/shard_map/rkc,drk->drc/dot_general | solution.py:59
  241.5 4.0 collective-permute-start.7
  245.5 3.3 collective-permute-start.13
  253.0 5.7 collective-permute-done.8
  263.5 5.5 collective-permute-start.11
  270.5 2.9 collective-permute-start.12
  277.4 6.9 %copy_bitcast_fusion.2 = f32[16,64,128]{2,0,1:T(8,128)S(1)} fusion(f32[16,8192]{1,0:T(8,128)S(1)} %bitcast_multiply_fusion.1, f32[8,8192]{1,0:T(8,128)S(1)} %collective-permute-done.14, f32[8,8192]{1,0:T(8,128)S(1)} %collective-permute-done.13, f32[]{:T(128)} %bitcast.13, f32[]{:T(128)} %bitcast.12, f32[]{:T(128)} %bitcast.11, f32[]{:T(128)} %bitcast.10, ...), kind=kLoop, calls=%fused_computation.370 | loop fusion | flops 5373952 | bytes 1572900 | tf_op jit(solution)/shard_map/reshape | solution.py:57
  284.3 3.1 gather_fusion.4
  287.4 45.1 %fusion.2 = f32[64,16,128]{2,1,0:T(8,128)S(1)} fusion(f32[64,1024]{1,0:T(8,128)S(1)} %get-tuple-element.43, f32[64,128]{1,0:T(8,128)S(1)} %bitcast.227, f32[64,1024]{1,0:T(8,128)} %get-tuple-element.44, f32[64,128]{1,0:T(8,128)S(1)} %bitcast.221, f32[64,8,2,8,128]{4,3,2,1,0:T(8,128)} %bitcast.204), kind=kOutput, calls=%fused_computation.10 | convolution fusion | flops 922746880 | bytes 5308416 | tf_op jit(solution)/shard_map/rkc,drk->drc/dot_general | solution.py:59
  337.6 3.6 collective-permute-done.15
  341.9 5.1 collective-permute-done.16
  347.8 3.6 collective-permute-done.17
  352.5 3.6 collective-permute-done.19
  356.1 3.5 collective-permute-start.20
  371.5 3.0 slice_bitcast_fusion
  374.5 3.8 collective-permute-done.23
  378.3 6.9 %copy_bitcast_fusion.1 = f32[16,64,128]{2,0,1:T(8,128)S(1)} fusion(f32[16,8192]{1,0:T(8,128)S(1)} %fusion.213, f32[8,8192]{1,0:T(8,128)S(1)} %collective-permute-done.23, f32[8,8192]{1,0:T(8,128)S(1)} %collective-permute-done.22, f32[]{:T(128)} %bitcast.13, f32[]{:T(128)} %bitcast.12, f32[]{:T(128)} %bitcast.11, f32[]{:T(128)} %bitcast.10, f32[]{:T(128)} %bitcast.9, ...), kind=kLoop, calls=%fused_computation.369 | loop fusion | flops 5373952 | bytes 1572900 | tf_op jit(solution)/shard_map/reshape | solution.py:57
  385.2 3.1 gather_fusion.5
  388.3 46.6 %fusion.25 = (f32[]{:T(128)}, f32[64,16,128]{2,1,0:T(8,128)S(1)}) fusion(f32[64,16,128]{2,1,0:T(8,128)S(1)} %fusion.18, f32[64,1024]{1,0:T(8,128)S(1)} %get-tuple-element.43, f32[64,128]{1,0:T(8,128)S(1)} %bitcast.228, f32[64,1024]{1,0:T(8,128)} %get-tuple-element.44, f32[64,128]{1,0:T(8,128)S(1)} %bitcast.222, f32[64,8,2,8,128]{4,3,2,1,0:T(8,128)} %bitcast.202), kind=kOutput, calls=%fused_computation.173 | convolution fusion | flops 923140096 | bytes 5832708 | tf_op jit(solution)/shard_map/rkc,drk->drc/dot_general | solution.py:59
  437.2 4.6 collective-permute-start.31
  443.1 6.2 %collective-permute-start.25 = (f32[1,128]{1,0:T(1,128)S(1)}, f32[1,128]{1,0:T(1,128)S(1)}, u32[]{:S(2)}, u32[]{:S(2)}) collective-permute-start(f32[1,128]{1,0:T(1,128)S(1)} %broadcast_add_fusion.1), channel_id=1, source_target_pairs={{0,32},{16,48},{32,0},{48,16},{64,96},{80,112},{96,64},{112,80},{1... | collective-permute-start | bytes 1544 | tf_op jit(solution)/shard_map/ppermute | solution.py:77
  459.7 5.5 collective-permute-start.29
  466.8 5.3 collective-permute-start.30
  473.8 9.6 %copy_bitcast_fusion = f32[16,64,128]{2,0,1:T(8,128)S(1)} fusion(f32[16,8192]{1,0:T(8,128)S(1)} %bitcast_multiply_fusion, f32[8,8192]{1,0:T(8,128)} %collective-permute-done.32, f32[8,8192]{1,0:T(8,128)} %collective-permute-done.31, f32[]{:T(128)} %bitcast.13, f32[]{:T(128)} %bitcast.12, f32[]{:T(128)} %bitcast.11, f32[]{:T(128)} %bitcast.10, f32[]{:T(128)} %bitcast.9, ...), kind=kLoop, calls=%fused_computation.368 | loop fusion | flops 5373952 | bytes 1572900 | tf_op jit(solution)/shard_map/reshape | solution.py:57
  483.3 3.1 gather_fusion.6
  486.4 45.1 %fusion.21 = f32[16,64,128]{2,0,1:T(8,128)S(1)} fusion(f32[64,1024]{1,0:T(8,128)S(1)} %get-tuple-element.43, f32[64,128]{1,0:T(8,128)S(1)} %bitcast.229, f32[64,1024]{1,0:T(8,128)} %get-tuple-element.44, f32[64,128]{1,0:T(8,128)S(1)} %bitcast.223, f32[64,8,2,8,128]{4,3,2,1,0:T(8,128)} %bitcast.199), kind=kOutput, calls=%fused_computation.167 | convolution fusion | flops 922746880 | bytes 5308416 | tf_op jit(solution)/shard_map/rkc,drk->drc/dot_general | solution.py:59
  532.2 7.8 %copy.89 = f32[2,16,8192]{1,0,2:T(2,128)} copy(f32[2,16,8192]{2,1,0:T(8,128)S(1)} %pad_maximum_fusion.1) | data formatting | bytes 2097152 | tf_op jit(solution)/shard_map/stack | solution.py:114
  540.0 12.9 %reshape.299 = f32[8,1,32768]{2,1,0:T(1,128)S(1)} reshape(f32[8192,2,16]{2,1,0:T(2,128)} %bitcast.187) | data formatting | bytes 2097152
  552.9 15.7 %all_to_all.30 = f32[8,1,32768]{2,1,0:T(1,128)S(1)} all-to-all(f32[8,1,32768]{2,1,0:T(1,128)S(1)} %reshape.299), channel_id=1, replica_groups=mesh['space'=8,'tm'=16] {'space'}, dimensions={0} | all-to-all | bytes 2097152 | tf_op jit(solution)/shard_map/all_to_all | solution.py:68
  569.1 3.2 reduce.13
  572.3 14.3 %reshape.300 = f32[8192,2,16]{2,1,0:T(2,128)} reshape(f32[8,32768]{1,0:T(8,128)S(1)} %reduce.13) | data formatting | bytes 2097152
  586.6 6.7 %copy.99 = f32[2,16,8,1024]{3,2,1,0:T(8,128)S(1)} copy(f32[2,16,8,1024]{1,0,3,2:T(2,128)} %bitcast.188) | data formatting | bytes 2097152 | tf_op jit(solution)/shard_map/all_to_all | solution.py:68
  (135 shorter events, 80.2 us)
Async XLA Ops:
  0.6 15.4 %copy-start.7 = (f32[9]{0:T(128)S(1)}, f32[9]{0:T(128)}, u32[]{:S(2)}) copy-start(f32[9]{0:T(128)} %param.9) | copy-start | bytes 112
  5.4 21.2 %all-to-all-start = ((f32[2,128,1024]{2,0,1:T(2,128)}), f32[2,128,1024]{2,0,1:T(2,128)S(1)}, u32[]{:S(2)}, u32[]{:S(2)}) async-start(f32[2,128,1024]{2,0,1:T(2,128)} %pad_maximum_fusion), calls=%async_computation | async-start | bytes 2097152 | tf_op jit(solution)/shard_map/all_to_all | solution.py:64
  27.1 7.6 %collective-permute-start = (f32[8,8192]{1,0:T(8,128)S(1)}, f32[8,8192]{1,0:T(8,128)S(1)}, u32[]{:S(2)}, u32[]{:S(2)}) collective-permute-start(f32[8,8192]{1,0:T(8,128)S(1)} %bitcast.217), channel_id=1, source_target_pairs={{0,16},{16,32},{32,48},{48,64},{64,80},{80,96},{96,112},{112,1},{1... | collective-permute-start | bytes 786440 | tf_op jit(solution)/shard_map/ppermute | solution.py:38
  30.0 9.0 %collective-permute-start.1 = (f32[8,8192]{1,0:T(8,128)S(1)}, f32[8,8192]{1,0:T(8,128)S(1)}, u32[]{:S(2)}, u32[]{:S(2)}) collective-permute-start(f32[8,8192]{1,0:T(8,128)S(1)} %bitcast.216), channel_id=1, source_target_pairs={{16,0},{32,16},{48,32},{64,48},{80,64},{96,80},{112,96},{1,112},{1... | collective-permute-start | bytes 786440 | tf_op jit(solution)/shard_map/ppermute | solution.py:39
  39.0 9.6 %copy-start.6 = (f32[64,1024]{1,0:T(8,128)S(1)}, f32[64,1024]{1,0:T(8,128)}, u32[]{:S(2)}) copy-start(f32[64,1024]{1,0:T(8,128)} %get-tuple-element.44) | copy-start | bytes 786436
  93.3 6.9 %collective-permute-start.2 = (f32[8,8192]{1,0:T(8,128)S(1)}, f32[8,8192]{1,0:T(8,128)S(1)}, u32[]{:S(2)}, u32[]{:S(2)}) collective-permute-start(f32[8,8192]{1,0:T(8,128)S(1)} %get-tuple-element.22), channel_id=1, source_target_pairs={{0,16},{16,32},{32,48},{48,64},{64,80},{80,96},{96,112},{112,1},{1... | collective-permute-start | bytes 786440 | tf_op jit(solution)/shard_map/ppermute | solution.py:38
  95.8 9.9 %collective-permute-start.3 = (f32[8,8192]{1,0:T(8,128)S(1)}, f32[8,8192]{1,0:T(8,128)S(1)}, u32[]{:S(2)}, u32[]{:S(2)}) collective-permute-start(f32[8,8192]{1,0:T(8,128)S(1)} %get-tuple-element.23), channel_id=1, source_target_pairs={{16,0},{32,16},{48,32},{64,48},{80,64},{96,80},{112,96},{1,112},{1... | collective-permute-start | bytes 786440 | tf_op jit(solution)/shard_map/ppermute | solution.py:39
  161.7 9.7 %collective-permute-start.4 = (f32[8,8192]{1,0:T(8,128)}, f32[8,8192]{1,0:T(8,128)}, u32[]{:S(2)}, u32[]{:S(2)}) collective-permute-start(f32[8,8192]{1,0:T(8,128)} %get-tuple-element.20), channel_id=1, source_target_pairs={{0,16},{16,32},{32,48},{48,64},{64,80},{80,96},{96,112},{112,1},{1... | collective-permute-start | bytes 786440 | tf_op jit(solution)/shard_map/ppermute | solution.py:38
  167.9 8.6 %collective-permute-start.5 = (f32[8,8192]{1,0:T(8,128)}, f32[8,8192]{1,0:T(8,128)}, u32[]{:S(2)}, u32[]{:S(2)}) collective-permute-start(f32[8,8192]{1,0:T(8,128)} %get-tuple-element.21), channel_id=1, source_target_pairs={{16,0},{32,16},{48,32},{64,48},{80,64},{96,80},{112,96},{1,112},{1... | collective-permute-start | bytes 786440 | tf_op jit(solution)/shard_map/ppermute | solution.py:39
  169.8 1.6 copy-start
  237.8 3.6 collective-permute-start.6
  241.5 8.7 %collective-permute-start.7 = (f32[2,128]{1,0:T(2,128)S(1)}, f32[2,128]{1,0:T(2,128)S(1)}, u32[]{:S(2)}, u32[]{:S(2)}) collective-permute-start(f32[2,128]{1,0:T(2,128)S(1)} %broadcast_add_fusion), channel_id=1, source_target_pairs={{0,32},{16,48},{32,0},{48,16},{64,96},{80,112},{96,64},{112,80},{1... | collective-permute-start | bytes 3080 | tf_op jit(solution)/shard_map/ppermute | solution.py:77
  245.5 31.9 %collective-permute-start.13 = (f32[8,8192]{1,0:T(8,128)S(1)}, f32[8,8192]{1,0:T(8,128)S(1)}, u32[]{:S(2)}, u32[]{:S(2)}) collective-permute-start(f32[8,8192]{1,0:T(8,128)S(1)} %get-tuple-element.18), channel_id=1, source_target_pairs={{0,16},{16,32},{32,48},{48,64},{64,80},{80,96},{96,112},{112,1},{1... | collective-permute-start | bytes 786440 | tf_op jit(solution)/shard_map/ppermute | solution.py:38
  248.8 28.6 %collective-permute-start.14 = (f32[8,8192]{1,0:T(8,128)S(1)}, f32[8,8192]{1,0:T(8,128)S(1)}, u32[]{:S(2)}, u32[]{:S(2)}) collective-permute-start(f32[8,8192]{1,0:T(8,128)S(1)} %get-tuple-element.19), channel_id=1, source_target_pairs={{16,0},{32,16},{48,32},{64,48},{80,64},{96,80},{112,96},{1,112},{1... | collective-permute-start | bytes 786440 | tf_op jit(solution)/shard_map/ppermute | solution.py:39
  250.2 8.5 %collective-permute-start.8 = (f32[2,128]{1,0:T(2,128)S(1)}, f32[2,128]{1,0:T(2,128)S(1)}, u32[]{:S(2)}, u32[]{:S(2)}) collective-permute-start(f32[2,128]{1,0:T(2,128)S(1)} %fusion.287), channel_id=1, source_target_pairs={{0,64},{16,80},{32,96},{48,112},{64,0},{80,16},{96,32},{112,48},{1... | collective-permute-start | bytes 3080 | tf_op jit(solution)/shard_map/ppermute | solution.py:77
  258.7 1.2 collective-permute-start.9
  259.9 3.6 collective-permute-start.10
  263.5 7.0 %collective-permute-start.11 = (f32[2,128]{1,0:T(2,128)S(1)}, f32[2,128]{1,0:T(2,128)S(1)}, u32[]{:S(2)}, u32[]{:S(2)}) collective-permute-start(f32[2,128]{1,0:T(2,128)S(1)} %add.512), channel_id=1, source_target_pairs={{0,4},{1,5},{2,6},{3,7},{4,0},{5,1},{6,2},{7,3},{8,12},{9,13},{10,... | collective-permute-start | bytes 3080 | tf_op jit(solution)/shard_map/ppermute | solution.py:77
  270.5 5.1 collective-permute-start.12
  332.6 0.8 copy-start.5
  333.5 41.0 %copy-start.2 = (f32[16,64,128]{2,1,0:T(8,128)}, f32[16,64,128]{2,1,0:T(8,128)S(1)}, u32[]{:S(2)}) copy-start(f32[16,64,128]{2,1,0:T(8,128)S(1)} %copy.77) | copy-start | bytes 1572868
  337.5 3.6 collective-permute-start.15
  341.8 5.2 collective-permute-start.16
  347.7 3.6 collective-permute-start.17
  351.3 1.2 collective-permute-start.18
  352.5 3.6 collective-permute-start.19
  356.1 5.1 collective-permute-start.20
  361.2 5.1 collective-permute-start.21
  368.1 6.4 %collective-permute-start.22 = (f32[8,8192]{1,0:T(8,128)S(1)}, f32[8,8192]{1,0:T(8,128)S(1)}, u32[]{:S(2)}, u32[]{:S(2)}) collective-permute-start(f32[8,8192]{1,0:T(8,128)S(1)} %get-tuple-element.16), channel_id=1, source_target_pairs={{0,16},{16,32},{32,48},{48,64},{64,80},{80,96},{96,112},{112,1},{1... | collective-permute-start | bytes 786440 | tf_op jit(solution)/shard_map/ppermute | solution.py:38
  370.0 8.3 %collective-permute-start.23 = (f32[8,8192]{1,0:T(8,128)S(1)}, f32[8,8192]{1,0:T(8,128)S(1)}, u32[]{:S(2)}, u32[]{:S(2)}) collective-permute-start(f32[8,8192]{1,0:T(8,128)S(1)} %get-tuple-element.17), channel_id=1, source_target_pairs={{16,0},{32,16},{48,32},{64,48},{80,64},{96,80},{112,96},{1,112},{1... | collective-permute-start | bytes 786440 | tf_op jit(solution)/shard_map/ppermute | solution.py:39
  388.3 83.8 %copy-start.1 = (f32[16,64,128]{2,1,0:T(8,128)S(1)}, f32[16,64,128]{2,1,0:T(8,128)}, u32[]{:S(2)}) copy-start(f32[16,64,128]{2,1,0:T(8,128)} %copy-done) | copy-start | bytes 1572868
  388.3 83.9 %copy-start.3 = (f32[16,64,128]{2,1,0:T(8,128)S(1)}, f32[16,64,128]{2,1,0:T(8,128)}, u32[]{:S(2)}) copy-start(f32[16,64,128]{2,1,0:T(8,128)} %copy-done.2) | copy-start | bytes 1572868
  388.3 84.0 %copy-start.4 = (f32[1,8,2,8,1024]{4,3,2,1,0:T(8,128)S(1)}, f32[1,8,2,8,1024]{4,3,2,1,0:T(8,128)}, u32[]{:S(2)}) copy-start(f32[1,8,2,8,1024]{4,3,2,1,0:T(8,128)} %get-tuple-element.8) | copy-start | bytes 1572868
  436.3 6.8 %collective-permute-start.24 = (f32[1,128]{1,0:T(1,128)S(1)}, f32[1,128]{1,0:T(1,128)S(1)}, u32[]{:S(2)}, u32[]{:S(2)}) collective-permute-start(f32[1,128]{1,0:T(1,128)S(1)} %broadcast_in_dim.11), channel_id=1, source_target_pairs={{0,16},{16,0},{32,48},{48,32},{64,80},{80,64},{96,112},{112,96},{1... | collective-permute-start | bytes 1544 | tf_op jit(solution)/shard_map/ppermute | solution.py:77
  437.2 36.5 %collective-permute-start.31 = (f32[8,8192]{1,0:T(8,128)}, f32[8,8192]{1,0:T(8,128)}, u32[]{:S(2)}, u32[]{:S(2)}) collective-permute-start(f32[8,8192]{1,0:T(8,128)} %get-tuple-element.14), channel_id=1, source_target_pairs={{0,16},{16,32},{32,48},{48,64},{64,80},{80,96},{96,112},{112,1},{1... | collective-permute-start | bytes 786440 | tf_op jit(solution)/shard_map/ppermute | solution.py:38
  441.8 31.9 %collective-permute-start.32 = (f32[8,8192]{1,0:T(8,128)}, f32[8,8192]{1,0:T(8,128)}, u32[]{:S(2)}, u32[]{:S(2)}) collective-permute-start(f32[8,8192]{1,0:T(8,128)} %get-tuple-element.15), channel_id=1, source_target_pairs={{16,0},{32,16},{48,32},{64,48},{80,64},{96,80},{112,96},{1,112},{1... | collective-permute-start | bytes 786440 | tf_op jit(solution)/shard_map/ppermute | solution.py:39
  443.1 7.8 %collective-permute-start.25 = (f32[1,128]{1,0:T(1,128)S(1)}, f32[1,128]{1,0:T(1,128)S(1)}, u32[]{:S(2)}, u32[]{:S(2)}) collective-permute-start(f32[1,128]{1,0:T(1,128)S(1)} %broadcast_add_fusion.1), channel_id=1, source_target_pairs={{0,32},{16,48},{32,0},{48,16},{64,96},{80,112},{96,64},{112,80},{1... | collective-permute-start | bytes 1544 | tf_op jit(solution)/shard_map/ppermute | solution.py:77
  450.9 3.6 collective-permute-start.26
  454.5 1.2 collective-permute-start.27
  455.7 4.0 collective-permute-start.28
  459.7 7.1 %collective-permute-start.29 = (f32[1,128]{1,0:T(1,128)S(1)}, f32[1,128]{1,0:T(1,128)S(1)}, u32[]{:S(2)}, u32[]{:S(2)}) collective-permute-start(f32[1,128]{1,0:T(1,128)S(1)} %add.564), channel_id=1, source_target_pairs={{0,4},{1,5},{2,6},{3,7},{4,0},{5,1},{6,2},{7,3},{8,12},{9,13},{10,... | collective-permute-start | bytes 1544 | tf_op jit(solution)/shard_map/ppermute | solution.py:77
  466.8 6.9 %collective-permute-start.30 = (f32[1,128]{1,0:T(1,128)S(1)}, f32[1,128]{1,0:T(1,128)S(1)}, u32[]{:S(2)}, u32[]{:S(2)}) collective-permute-start(f32[1,128]{1,0:T(1,128)S(1)} %add.565), channel_id=1, source_target_pairs={{0,8},{1,9},{2,10},{3,11},{4,12},{5,13},{6,14},{7,15},{8,0},{9,1},... | collective-permute-start | bytes 1544 | tf_op jit(solution)/shard_map/ppermute | solution.py:77
